TPU v7x, 32 devices: a whole 2x2x4 slice. The times are simulated.
32 devices in a mesh: dp: 8 (over y, x, core), tensor: 4 (over z).
Axes of the slice: x: 2, y: 2, z: 4, core: 2. Of those that a mesh axis runs over, the one named last changes fastest.
Arguments:
- block_input: bfloat16 [4096, 1024], P('dp'), may hold values from -6 to 6
- cotangent: bfloat16 [4096, 1024], P('dp'), may hold values from -6 to 6
- seq_lengths: int32 [8, 4], P('dp'), may hold values from 0 to 512, as said below
- norm_gains: float32 [2, 2, 1024], replicated, may hold values from 0.1 to 1.9
- norm_biases: float32 [2, 2, 1024], replicated, may hold values from -3 to 3
- w_qkv: bfloat16 [2, 1024, 3, 1024], P(None, None, None, 'tensor'), may hold values from -0.1875 to 0.1875
- qv_bias: float32 [2, 2, 1024], P(None, None, 'tensor'), may hold values from -3 to 3
- w_out: bfloat16 [2, 1024, 1024], P(None, 'tensor'), may hold values from -0.375 to 0.375
- out_biases: float32 [2, 2, 1024], replicated, may hold values from -3 to 3
- w_up: bfloat16 [2, 1024, 4096], P(None, None, 'tensor'), may hold values from -0.1875 to 0.1875
- up_bias: float32 [2, 4096], P(None, 'tensor'), may hold values from -3 to 3
- w_down: bfloat16 [2, 4096, 1024], P(None, 'tensor'), may hold values from -0.09375 to 0.09375
Outputs:
- block_output: bfloat16 [4096, 1024], P('dp')
- input_grad: float32 [4096, 1024], P('dp')
- grad_norm_gains: float32 [2, 2, 1024], replicated
- grad_norm_biases: float32 [2, 2, 1024], replicated
- grad_w_qkv: float32 [2, 1024, 3, 1024], P(None, 'dp', None, 'tensor')
- grad_qv_bias: float32 [2, 2, 1024], P(None, None, 'tensor')
- grad_w_out: float32 [2, 1024, 1024], P(None, 'tensor', 'dp')
- grad_out_biases: float32 [2, 2, 1024], replicated
- grad_w_up: float32 [2, 1024, 4096], P(None, 'dp', 'tensor')
- grad_up_bias: float32 [2, 4096], P(None, 'tensor')
- grad_w_down: float32 [2, 4096, 1024], P(None, 'tensor', 'dp')
Inputs may be any that keep to these rules, and one draw needn't show every extreme that they name: `seq_lengths`: each row's lengths sum to at most 512; zero lengths occur; in every draw one row holds a single sequence of exactly 512 tokens.
All inputs are finite; a program needn't handle non-finite values.
Results may differ from a plain program's by a relative error of at most 0.025.
Values may be sent and summed in bfloat16 or wider, within the bound.
A program may use at most 128 MiB of HBM per device.

v0:
```python
import jax
import jax.numpy as jnp
from jax import lax
from jax.sharding import PartitionSpec as P

HEADS = 16
HEAD_DIM = 64
NORM_EPS = 1e-05


def layer_norm(residual, gain_vec, shift_vec):
    mean_row = jnp.mean(residual, axis=-1, keepdims=True)
    centered = residual - mean_row
    variance = jnp.mean(centered * centered, axis=-1, keepdims=True)
    return centered * lax.rsqrt(variance + NORM_EPS) * gain_vec + shift_vec


def gelu_tanh(pre_act):
    return (
        0.5
        * pre_act
        * (1.0 + jnp.tanh(0.7978845608028654 * (pre_act + 0.044715 * pre_act * pre_act * pre_act)))
    )


def norm_back(residual, gain_vec, shift_vec, grad_normed):
    result, pull_back = jax.vjp(layer_norm, residual, gain_vec, shift_vec)
    return pull_back(grad_normed)


def segment_mask(lengths, row_count):
    seq_ends = jnp.cumsum(lengths)
    position = jnp.arange(row_count, dtype=jnp.int32)
    segment = jnp.sum((position[:, None] >= seq_ends[None, :]).astype(jnp.int32), axis=1)
    same_seq = (segment[:, None] == segment[None, :]) & (position[None, :] <= position[:, None])
    row_gap = (position[:, None] - position[None, :]).astype(jnp.float32)
    live_rows = (position < seq_ends[-1]).astype(jnp.float32)
    return (same_seq, row_gap, live_rows)


def on_device(
    block_input,
    cotangent,
    seq_lengths,
    norm_gains,
    norm_biases,
    w_qkv,
    qv_bias,
    w_out,
    out_biases,
    w_up,
    up_bias,
    w_down,
):
    row_count = block_input.shape[0]
    my_rank = lax.axis_index("tensor")
    local_width = w_qkv.shape[3]
    heads_here = local_width // HEAD_DIM
    depth = w_qkv.shape[0]
    score_scale = HEAD_DIM ** (-0.5)
    f32 = jnp.float32
    same_seq, row_gap, live_rows = segment_mask(seq_lengths[0], row_count)
    head_index = my_rank * heads_here + jnp.arange(heads_here, dtype=jnp.int32) + 1
    slopes = jnp.exp2(-8.0 * head_index.astype(f32) / HEADS)

    def branch_total(partial_value):
        return lax.psum(partial_value.astype(jnp.bfloat16), "tensor").astype(jnp.float32)

    def input_total(partial_value):
        return lax.psum(partial_value.astype(jnp.bfloat16), "tensor").astype(jnp.float32)

    def score_block(queries, key_rows):
        raw_scores = (
            jnp.einsum("the,she->hts", queries, key_rows, preferred_element_type=f32) * score_scale
        )
        raw_scores = raw_scores - slopes[:, None, None] * row_gap
        return jnp.where(same_seq, raw_scores, -1000000000.0)

    head_shape = (row_count, heads_here, HEAD_DIM)
    residual = block_input.astype(f32)
    stored = []
    for layer_idx in range(depth):
        entering = residual
        normed = layer_norm(residual, norm_gains[layer_idx, 0], norm_biases[layer_idx, 0]).astype(
            jnp.bfloat16
        )
        projected = jnp.einsum("td,dcn->tcn", normed, w_qkv[layer_idx], preferred_element_type=f32)
        queries = (projected[:, 0] + qv_bias[layer_idx, 0]).astype(jnp.bfloat16).reshape(head_shape)
        key_rows = projected[:, 1].astype(jnp.bfloat16).reshape(head_shape)
        value_rows = (
            (projected[:, 2] + qv_bias[layer_idx, 1]).astype(jnp.bfloat16).reshape(head_shape)
        )
        scores = score_block(queries, key_rows)
        row_max = jnp.max(scores, axis=-1, keepdims=True)
        log_total = row_max + jnp.log(jnp.sum(jnp.exp(scores - row_max), axis=-1, keepdims=True))
        softmax_p = jnp.exp(scores - log_total).astype(jnp.bfloat16)
        context = jnp.einsum("hts,she->the", softmax_p, value_rows, preferred_element_type=f32)
        context = context.astype(jnp.bfloat16).reshape(row_count, local_width)
        partial_value = jnp.dot(context, w_out[layer_idx], preferred_element_type=f32)
        residual = residual + branch_total(partial_value) + out_biases[layer_idx, 0]
        middle = residual
        normed_mlp = layer_norm(
            residual, norm_gains[layer_idx, 1], norm_biases[layer_idx, 1]
        ).astype(jnp.bfloat16)
        up_proj = (
            jnp.dot(normed_mlp, w_up[layer_idx], preferred_element_type=f32) + up_bias[layer_idx]
        )
        activated = gelu_tanh(up_proj).astype(jnp.bfloat16)
        partial_value = jnp.dot(activated, w_down[layer_idx], preferred_element_type=f32)
        residual = residual + branch_total(partial_value) + out_biases[layer_idx, 1]
        stored.append(
            (
                entering,
                normed,
                queries,
                key_rows,
                value_rows,
                log_total,
                context,
                middle,
                normed_mlp,
                up_proj,
                activated,
            )
        )
    block_rows = residual.astype(jnp.bfloat16)
    grad_rows = cotangent.astype(f32) * live_rows[:, None]
    small_parts = []
    heavy_parts = []
    for layer_idx in reversed(range(depth)):
        (
            entering,
            normed,
            queries,
            key_rows,
            value_rows,
            log_total,
            context,
            middle,
            normed_mlp,
            up_proj,
            activated,
        ) = stored[layer_idx]
        down_bias_grad = jnp.sum(grad_rows, axis=0)
        grad_low = grad_rows.astype(jnp.bfloat16)
        down_w_grad = jnp.einsum("tf,td->fd", activated, grad_low, preferred_element_type=f32)
        act_grad = jnp.einsum("td,fd->tf", grad_low, w_down[layer_idx], preferred_element_type=f32)
        up_grad = jax.vjp(gelu_tanh, up_proj)[1](act_grad)[0].astype(jnp.bfloat16)
        up_bias_grad = jnp.sum(up_grad.astype(f32), axis=0)
        up_w_grad = jnp.einsum("td,tf->df", normed_mlp, up_grad, preferred_element_type=f32)
        normed_grad = input_total(
            jnp.einsum("tf,df->td", up_grad, w_up[layer_idx], preferred_element_type=f32)
        )
        middle_grad, gain_mlp, shift_mlp = norm_back(
            middle, norm_gains[layer_idx, 1], norm_biases[layer_idx, 1], normed_grad
        )
        grad_rows = grad_rows + middle_grad
        out_bias_grad = jnp.sum(grad_rows, axis=0)
        grad_low = grad_rows.astype(jnp.bfloat16)
        out_w_grad = jnp.einsum("tn,td->nd", context, grad_low, preferred_element_type=f32)
        context_grad = jnp.einsum(
            "td,nd->tn", grad_low, w_out[layer_idx], preferred_element_type=f32
        )
        context_grad = context_grad.astype(jnp.bfloat16).reshape(head_shape)
        scores = score_block(queries, key_rows)
        softmax_f = jnp.exp(scores - log_total)
        prob_grad = jnp.einsum("the,she->hts", context_grad, value_rows, preferred_element_type=f32)
        score_grad = softmax_f * (
            prob_grad - jnp.sum(prob_grad * softmax_f, axis=-1, keepdims=True)
        )
        score_grad = score_grad.astype(jnp.bfloat16)
        query_grad = (
            jnp.einsum("hts,she->the", score_grad, key_rows, preferred_element_type=f32)
            * score_scale
        )
        key_grad = (
            jnp.einsum("hts,the->she", score_grad, queries, preferred_element_type=f32)
            * score_scale
        )
        value_grad = jnp.einsum(
            "hts,the->she", softmax_f.astype(jnp.bfloat16), context_grad, preferred_element_type=f32
        )
        qkv_grad = (
            jnp.stack([query_grad, key_grad, value_grad], axis=1)
            .astype(jnp.bfloat16)
            .reshape(row_count, 3, local_width)
        )
        qkv_w_grad = jnp.einsum("td,tcn->dcn", normed, qkv_grad, preferred_element_type=f32)
        qv_bias_grad = jnp.sum(qkv_grad[:, 0::2].astype(f32), axis=0)
        normed_grad = input_total(
            jnp.einsum("tcn,dcn->td", qkv_grad, w_qkv[layer_idx], preferred_element_type=f32)
        )
        enter_grad, gain_attn, shift_attn = norm_back(
            entering, norm_gains[layer_idx, 0], norm_biases[layer_idx, 0], normed_grad
        )
        grad_rows = grad_rows + enter_grad
        small_parts.append(
            (
                jnp.stack([gain_attn, gain_mlp]),
                jnp.stack([shift_attn, shift_mlp]),
                jnp.stack([out_bias_grad, down_bias_grad]),
                qv_bias_grad,
                up_bias_grad,
            )
        )
        heavy = (qkv_w_grad, out_w_grad, up_w_grad, down_w_grad)
        heavy_parts.append(heavy)
    small_parts = small_parts[::-1]
    heavy_parts = heavy_parts[::-1]
    gain_grads = jnp.stack([entry[0] for entry in small_parts])
    shift_grads = jnp.stack([entry[1] for entry in small_parts])
    bias_grads = jnp.stack([entry[2] for entry in small_parts])
    qv_grads = jnp.stack([entry[3] for entry in small_parts])
    up_bias_grads = jnp.stack([entry[4] for entry in small_parts])
    gain_grads, shift_grads, bias_grads = (gain_grads, shift_grads, bias_grads)
    gain_grads, shift_grads, bias_grads, qv_grads, up_bias_grads = (
        lax.psum(gain_grads.astype(jnp.bfloat16), "dp").astype(jnp.float32),
        lax.psum(shift_grads.astype(jnp.bfloat16), "dp").astype(jnp.float32),
        lax.psum(bias_grads.astype(jnp.bfloat16), "dp").astype(jnp.float32),
        lax.psum(qv_grads.astype(jnp.bfloat16), "dp").astype(jnp.float32),
        lax.psum(up_bias_grads.astype(jnp.bfloat16), "dp").astype(jnp.float32),
    )
    qkv_all = jnp.stack([entry[0] for entry in heavy_parts])
    out_all = jnp.stack([entry[1] for entry in heavy_parts])
    up_all = jnp.stack([entry[2] for entry in heavy_parts])
    down_all = jnp.stack([entry[3] for entry in heavy_parts])
    qkv_all, out_all, up_all, down_all = (
        lax.psum_scatter(
            qkv_all.astype(jnp.bfloat16), "dp", scatter_dimension=1, tiled=True
        ).astype(jnp.float32),
        lax.psum_scatter(
            out_all.astype(jnp.bfloat16), "dp", scatter_dimension=2, tiled=True
        ).astype(jnp.float32),
        lax.psum_scatter(up_all.astype(jnp.bfloat16), "dp", scatter_dimension=1, tiled=True).astype(
            jnp.float32
        ),
        lax.psum_scatter(
            down_all.astype(jnp.bfloat16), "dp", scatter_dimension=2, tiled=True
        ).astype(jnp.float32),
    )
    return (
        block_rows,
        grad_rows,
        gain_grads,
        shift_grads,
        qkv_all,
        qv_grads,
        out_all,
        bias_grads,
        up_all,
        up_bias_grads,
        down_all,
    )


def solution(mesh):
    in_specs = (
        P("dp", None),
        P("dp", None),
        P("dp", None),
        P(),
        P(),
        P(None, None, None, "tensor"),
        P(None, None, "tensor"),
        P(None, "tensor", None),
        P(),
        P(None, None, "tensor"),
        P(None, "tensor"),
        P(None, "tensor", None),
    )
    out_specs = (
        P("dp", None),
        P("dp", None),
        P(),
        P(),
        P(None, "dp", None, "tensor"),
        P(None, None, "tensor"),
        P(None, "tensor", "dp"),
        P(),
        P(None, "dp", "tensor"),
        P(None, "tensor"),
        P(None, "tensor", "dp"),
    )
    return jax.shard_map(
        on_device, mesh=mesh, in_specs=in_specs, out_specs=out_specs, check_vma=False
    )
```

profile of v0, /device:TPU:0, one launch (start us, length us, event | category | flops | bytes accessed | tf_op | source)
XLA Modules:
  0.0 713.0 jit_solution(7808958398125200820)
XLA Ops:
  10.5 2.6 fusion.72
  15.1 2.7 fusion.153
  19.9 3.0 convolution_convert_fusion.11
  24.6 54.7 %all-reduce.10.cloned.1.call-done = bf16[512,1024]{1,0:T(8,128)(2,1)} async-done(((bf16[512,1024]{1,0:T(8,128)(2,1)}), bf16[512,1024]{1,0:T(8,128)(2,1)}) %all-reduce.10.cloned.1.call-update) | async-done | bytes 1048592 | tf_op jit(solution)/shard_map/psum | solution.py:67
  81.6 3.1 fusion.54
  86.1 2.5 fusion.77
  89.1 51.0 %all-reduce.12.cloned.1.call-done = bf16[512,1024]{1,0:T(8,128)(2,1)} async-done(((bf16[512,1024]{1,0:T(8,128)(2,1)}), bf16[512,1024]{1,0:T(8,128)(2,1)}) %all-reduce.12.cloned.1.call-update) | async-done | bytes 1048592 | tf_op jit(solution)/shard_map/psum | solution.py:67
  140.0 2.3 fusion.146
  153.1 50.0 %all-reduce.14.cloned.1.call-done = bf16[512,1024]{1,0:T(8,128)(2,1)} async-done(((bf16[512,1024]{1,0:T(8,128)(2,1)}), bf16[512,1024]{1,0:T(8,128)(2,1)}) %all-reduce.14.cloned.1.call-update) | async-done | bytes 1048592 | tf_op jit(solution)/shard_map/psum | solution.py:67
  203.2 2.4 fusion.145
  209.3 3.4 fusion.155
  213.7 2.3 fusion.80
  216.5 50.8 %all-reduce.16.cloned.1.call-done = bf16[512,1024]{1,0:T(8,128)(2,1)} async-done(((bf16[512,1024]{1,0:T(8,128)(2,1)}), bf16[512,1024]{1,0:T(8,128)(2,1)}) %all-reduce.16.cloned.1.call-update) | async-done | bytes 1048592 | tf_op jit(solution)/shard_map/psum | solution.py:70
  267.3 1.8 fusion.20
  280.1 1.8 copy.70
  285.5 3.6 bitcast_convert_fusion.1
  289.4 51.1 %all-reduce.18.cloned.1.call-done = bf16[512,1024]{1,0:T(8,128)(2,1)} async-done(((bf16[512,1024]{1,0:T(8,128)(2,1)}), bf16[512,1024]{1,0:T(8,128)(2,1)}) %all-reduce.18.cloned.1.call-update) | async-done | bytes 1048592 | tf_op jit(solution)/shard_map/psum | solution.py:70
  340.5 2.5 fusion.19
  345.5 2.2 copy-done.61
  348.3 3.6 fusion.156
  352.9 2.3 fusion.74
  355.3 4.8 fusion.83
  361.4 45.2 %all-reduce.20.cloned.1.call-done = bf16[512,1024]{1,0:T(8,128)(2,1)} async-done(((bf16[512,1024]{1,0:T(8,128)(2,1)}), bf16[512,1024]{1,0:T(8,128)(2,1)}) %all-reduce.20.cloned.1.call-update) | async-done | bytes 1048592 | tf_op jit(solution)/shard_map/psum | solution.py:70
  406.5 2.4 fusion.18
  415.7 3.7 copy.97
  419.3 2.5 copy.103
  422.1 3.6 multiply_reduce_fusion
  429.4 1.8 copy.77
  431.2 3.3 fusion.102
  436.3 3.7 convolution_convert_fusion.6
  441.7 3.6 bitcast_convert_fusion
  446.3 3.0 fusion.87
  450.5 2.0 pad_maximum_fusion.2
  452.9 3.8 convert_bitcast_fusion
  458.4 2.3 pad_maximum_fusion.1
  460.7 11.4 %copy.99 = bf16[2,1024,1024]{1,0,2:T(2,128)(2,1)} copy(bf16[2,1024,1024]{2,1,0:T(8,128)(2,1)} %pad_maximum_fusion.1) | data formatting | bytes 8388608
  472.1 5.6 copy.104
  477.8 2.8 convert_bitcast_fusion.2
  482.2 2.3 pad_maximum_fusion
  494.0 52.3 %all-reduce.22.cloned.1.call-done = (bf16[512,1024]{1,0:T(8,128)(2,1)}, bf16[512,1024]{1,0:T(8,128)(2,1)}) async-done(((bf16[512,1024]{1,0:T(8,128)(2,1)}, bf16[512,1024]{1,0:T(8,128)(2,1)}), (bf16[512,1024]{1,0:T(8,128)(2,1)}, bf16[512,1024]{1,0:T(8,128)(2,1)})) %all-reduce.22.cloned.1.call-update) | async-done | bytes 2097168 | tf_op jit(solution)/shard_map/psum | solution.py:67
  547.8 1.8 fusion.34
  551.0 24.5 %all-reduce = (bf16[2,2,1024]{2,1,0:T(2,128)(2,1)S(1)}, bf16[2,2,1024]{2,1,0:T(2,128)(2,1)S(1)}, bf16[2,2,256]{2,1,0:T(2,128)(2,1)S(1)}, bf16[2,2,1024]{2,1,0:T(2,128)(2,1)S(1)}, bf16[2,1024]{1,0:T(2,128)(2,1)S(1)}) all-reduce(bf16[2,2,1024]{2,1,0:T(2,128)(2,1)S(1)} %pad_maximum_fusion.6, ...), channel_id=1, replica_groups=mesh['dp'=8,'tensor'=4] {'dp'}, use_global_device_ids=true, to_apply=%region_36.37 | all-reduce | flops 15360 | bytes 61440 | tf_op jit(solution)/shard_map/psum | solution.py:217
  578.5 4.6 add_add_fusion.4
  583.2 11.8 %reduce-scatter.9.cloned.1.call-done = bf16[2,128,3,256]{3,1,2,0:T(8,128)(2,1)} async-done(((bf16[2,1024,3,256]{3,1,2,0:T(8,128)(2,1)}), bf16[2,128,3,256]{3,1,2,0:T(8,128)(2,1)}) %reduce-scatter.9.cloned.1.call-update) | async-done | bytes 393232 | tf_op jit(solution)/shard_map/reduce_scatter | solution.py:228
  594.9 1.9 convert_element_type.280
  596.9 52.4 %reduce-scatter.15.cloned.1.call-done = bf16[128,2048]{1,0:T(8,128)(2,1)} async-done(((bf16[1024,2048]{1,0:T(8,128)(2,1)}), bf16[128,2048]{1,0:T(8,128)(2,1)}) %reduce-scatter.15.cloned.1.call-update) | async-done | bytes 524304
  652.3 51.5 %reduce-scatter.11.cloned.1.call-done = bf16[2,128,1024]{2,1,0:T(8,128)(2,1)} async-done(((bf16[2,1024,1024]{2,1,0:T(8,128)(2,1)}), bf16[2,128,1024]{2,1,0:T(8,128)(2,1)}) %reduce-scatter.11.cloned.1.call-update) | async-done | bytes 524304 | tf_op jit(solution)/shard_map/reduce_scatter | solution.py:234
  703.8 2.1 convert_element_type.286
  (283 shorter events, 87.0 us)
Async XLA Ops:
  7.2 3.3 copy-start
  7.2 3.2 copy-start.50
  7.2 3.3 copy-start.51
  7.2 72.1 %all-reduce.10.cloned.1.call-start = ((), (), s32[]{:S(2)}) async-start(), calls=%async_computation.4 | async-start | bytes 2097152 | tf_op jit(solution)/shard_map/psum | solution.py:67
  13.2 4.7 copy-start.31
  13.2 6.7 copy-start.22
  13.3 4.6 copy-start.35
  15.1 2.8 copy-start.48
  19.9 3.1 copy-start.25
  24.5 115.5 %all-reduce.12.cloned.1.call-start = ((), (), s32[]{:S(2)}) async-start(), calls=%async_computation.5 | async-start | bytes 2097152 | tf_op jit(solution)/shard_map/psum | solution.py:67
  81.6 4.5 copy-start.59
  88.6 114.5 %all-reduce.14.cloned.1.call-start = ((), (), s32[]{:S(2)}) async-start(), calls=%async_computation.6 | async-start | bytes 2097152 | tf_op jit(solution)/shard_map/psum | solution.py:67
  140.0 2.7 copy-start.62
  144.1 3.1 copy-start.32
  144.1 3.8 copy-start.23
  144.1 3.1 copy-start.37
  149.9 53.2 %copy-start.29 = (bf16[4,64,512]{2,1,0:T(8,128)(2,1)}, bf16[4,64,512]{2,1,0:T(8,128)(2,1)S(1)}, u32[]{:S(2)}) copy-start(bf16[4,64,512]{2,1,0:T(8,128)(2,1)S(1)} %convolution_convert_fusion.10) | copy-start | bytes 786436
  151.9 115.5 %all-reduce.16.cloned.1.call-start = ((), (), s32[]{:S(2)}) async-start(), calls=%async_computation.7 | async-start | bytes 2097152 | tf_op jit(solution)/shard_map/psum | solution.py:70
  203.2 3.1 copy-start.57
  206.3 3.0 copy-start.60
  207.6 5.1 copy-start.68
  216.0 124.5 %all-reduce.18.cloned.1.call-start = ((), (), s32[]{:S(2)}) async-start(), calls=%async_computation.8 | async-start | bytes 2097152 | tf_op jit(solution)/shard_map/psum | solution.py:70
  270.3 3.3 copy-start.4
  289.2 117.4 %all-reduce.20.cloned.1.call-start = ((), (), s32[]{:S(2)}) async-start(), calls=%async_computation.9 | async-start | bytes 2097152 | tf_op jit(solution)/shard_map/psum | solution.py:70
  340.5 2.6 copy-start.6
  340.5 2.8 copy-start.17
  344.7 2.9 copy-start.61
  344.7 3.6 copy-start.65
  345.5 6.5 copy-start.19
  348.3 4.6 copy-start.58
  355.2 137.0 %reduce-scatter.13.cloned.1.call-start = ((), (), s32[]{:S(2)}) async-start(), calls=%async_computation.12 | async-start | bytes 1179648
  355.3 4.9 copy-start.12
  355.3 4.9 copy-start.30
  421.8 124.6 %all-reduce.22.cloned.1.call-start = ((), (), s32[]{:S(2)}) async-start(), calls=%async_computation.14 | async-start | bytes 4194304 | tf_op jit(solution)/shard_map/psum | solution.py:67
  422.1 3.6 copy-start.2
  425.7 2.5 copy-start.36
  445.3 149.6 %reduce-scatter.9.cloned.1.call-start = ((), (), s32[]{:S(2)}) async-start(), calls=%async_computation.10 | async-start | bytes 3538944 | tf_op jit(solution)/shard_map/reduce_scatter | solution.py:228
  446.3 3.0 copy-start.41
  446.3 3.0 copy-start.43
  446.3 3.0 copy-start.45
  452.6 196.7 %reduce-scatter.15.cloned.1.call-start = ((), (), s32[]{:S(2)}) async-start(), calls=%async_computation.13 | async-start | bytes 4718592
  452.9 3.9 copy-start.21
  452.9 3.9 copy-start.66
  477.7 226.1 %reduce-scatter.11.cloned.1.call-start = ((), (), s32[]{:S(2)}) async-start(), calls=%async_computation.11 | async-start | bytes 4718592 | tf_op jit(solution)/shard_map/reduce_scatter | solution.py:234
  477.8 2.9 copy-start.9
  477.8 2.9 copy-start.70
  484.6 3.4 copy-start.56
  487.8 3.1 copy-start.42
  (34 other events, 53.3 us)
Sparse Core Ops, SparseCore 0:
  24.6 54.6 all-reduce.9
  88.7 51.2 all-reduce.11
  152.0 51.1 all-reduce.13
  216.1 51.1 all-reduce.15
  289.3 51.1 all-reduce.17
  355.3 51.1 all-reduce.19
  421.9 35.2 reduce-scatter.12
  460.2 86.1 all-reduce.21
  549.8 45.1 reduce-scatter.8
  598.1 51.1 reduce-scatter.14
  652.7 51.1 reduce-scatter.10
where the time goes:
time: 721 us; the launch traced here: 713 us
  waiting for transfers between devices  471 us (65%)
  matrix products  78.9 us (11%)
  other arithmetic  62.7 us (9%)
  local copies, waits for them, and re-layouts  58.7 us (8%)
  blocking collectives  24.5 us (3%)
  between operations  15.4 us (2%)
    psum x4, waiting for transfers between devices, branch_total(): lax.psum(partial_value.astype(jnp.bfloat16), 'tensor').astype(jnp.float32)  208 us
    psum x3, waiting for transfers between devices, input_total(): lax.psum(partial_value.astype(jnp.bfloat16), 'tensor').astype(jnp.float32)  147 us
    unnamed x13, waiting for transfers between devices  52.6 us
    reduce_scatter x1, waiting for transfers between devices, on_device(): lax.psum_scatter(up_all.astype(jnp.bfloat16), 'dp', scatter_dimension=1,...  51.5 us
    unnamed x150, local copies, waits for them, and re-layouts  47.4 us
    psum x1, blocking collectives, on_device(): lax.psum(gain_grads.astype(jnp.bfloat16), 'dp').astype(jnp.float32)  24.5 us
    reduce_sum x12, other arithmetic, layer_norm(): return centered * lax.rsqrt(variance + NORM_EPS) * gain_vec + shift_vec  19.1 us
  transfers between devices with their start and end apart: 11, of which 10 were waited for; matrix products, arithmetic and copies ran while one was open for 13% of the time, Pallas kernels for 0%

commit v1 on v0

--- a/solution.py
+++ b/solution.py
@@ -6,6 +6,12 @@
 HEADS = 16
 HEAD_DIM = 64
 NORM_EPS = 1e-05
+
+
+def gather_and_add(shard, axis):
+    blocks = lax.all_gather(shard, axis, axis=0, tiled=False)
+    total = blocks.sum(axis=0)
+    return total
 
 
 def layer_norm(residual, gain_vec, shift_vec):
@@ -64,7 +70,7 @@
     slopes = jnp.exp2(-8.0 * head_index.astype(f32) / HEADS)
 
     def branch_total(partial_value):
-        return lax.psum(partial_value.astype(jnp.bfloat16), "tensor").astype(jnp.float32)
+        return gather_and_add(partial_value.astype(jnp.bfloat16), "tensor").astype(jnp.float32)
 
     def input_total(partial_value):
         return lax.psum(partial_value.astype(jnp.bfloat16), "tensor").astype(jnp.float32)

time: 721 us -> 869 us (1.21)
  waiting for transfers between devices: 471 us -> 617 us
  matrix products: 78.9 us -> 66.8 us
  other arithmetic: 62.7 us -> 73.4 us
    all_gather x0 -> x4, waiting for transfers between devices: none -> 318 us  [gather_and_add(): blocks = lax.all_gather(shard, axis, axis=0, tiled=False)]
    psum x4 -> x0, waiting for transfers between devices: 208 us -> none  [branch_total(): lax.psum(partial_value.astype(jnp.bfloat16), 'tensor').astype(jnp.float32)]
    reduce_scatter x1, waiting for transfers between devices: 11.8 us -> 47.5 us  [on_device(): lax.psum_scatter(qkv_all.astype(jnp.bfloat16), 'dp', scatter_dimension=1,...]
    reduce_sum x0 -> x4, other arithmetic: none -> 16.5 us  [gather_and_add(): total = blocks.sum(axis=0)]
    unnamed x150 -> x160, local copies, waits for them, and re-layouts: 47.4 us -> 48.9 us
    psum x3 -> x4, waiting for transfers between devices: 147 us -> 147 us  [input_total(): lax.psum(partial_value.astype(jnp.bfloat16), 'tensor').astype(jnp.float32)]
    unnamed x13 -> x14, waiting for transfers between devices: 52.6 us -> 52.8 us
  transfers between devices with their start and end apart: 11 -> 12, of which waited for: 10 -> 10; matrix products, arithmetic and copies ran while one was open for 13% -> 9% of each run, Pallas kernels for 0% -> 0%
where the time goes in v1:
time: 869 us; the launch traced here: 860 us
  waiting for transfers between devices  617 us (71%)
  other arithmetic  73.4 us (8%)
  matrix products  66.8 us (8%)
  local copies, waits for them, and re-layouts  60.9 us (7%)
  blocking collectives  24.7 us (3%)
  between operations  15.6 us (2%)
    all_gather x4, waiting for transfers between devices, gather_and_add(): blocks = lax.all_gather(shard, axis, axis=0, tiled=False)  318 us
    psum x4, waiting for transfers between devices, input_total(): lax.psum(partial_value.astype(jnp.bfloat16), 'tensor').astype(jnp.float32)  147 us
    unnamed x14, waiting for transfers between devices  52.8 us
    reduce_scatter x1, waiting for transfers between devices, on_device(): lax.psum_scatter(up_all.astype(jnp.bfloat16), 'dp', scatter_dimension=1,...  51.3 us
    unnamed x160, local copies, waits for them, and re-layouts  48.9 us
    reduce_scatter x1, waiting for transfers between devices, on_device(): lax.psum_scatter(qkv_all.astype(jnp.bfloat16), 'dp', scatter_dimension=1,...  47.5 us
    psum x1, blocking collectives, on_device(): lax.psum(gain_grads.astype(jnp.bfloat16), 'dp').astype(jnp.float32)  24.7 us
  transfers between devices with their start and end apart: 12, of which 10 were waited for; matrix products, arithmetic and copies ran while one was open for 9% of the time, Pallas kernels for 0%

profile of v1, /device:TPU:0, one launch (start us, length us, event | category | flops | bytes accessed | tf_op | source)
XLA Modules:
  0.0 860.1 jit_solution(16740213471466628782)
XLA Ops:
  7.4 1.9 convert_reduce_fusion
  9.9 2.6 fusion.72
  20.0 83.5 %all-gather.9.cloned.1.call-done = bf16[2048,1024]{1,0:T(8,128)(2,1)} async-done(((bf16[512,1024]{1,0:T(8,128)(2,1)}), bf16[2048,1024]{1,0:T(8,128)(2,1)}) %all-gather.9.cloned.1.call-update) | async-done | bytes 4194320 | tf_op jit(solution)/shard_map/all_gather | solution.py:12
  103.5 3.3 reduce_sum.386
  112.2 2.5 fusion.77
  115.5 78.6 %all-gather.11.cloned.1.call-done = bf16[2048,1024]{1,0:T(8,128)(2,1)} async-done(((bf16[512,1024]{1,0:T(8,128)(2,1)}), bf16[2048,1024]{1,0:T(8,128)(2,1)}) %all-gather.11.cloned.1.call-update) | async-done | bytes 4194320 | tf_op jit(solution)/shard_map/all_gather | solution.py:12
  194.1 4.4 reduce_sum.392
  198.5 2.3 fusion.146
  212.0 77.9 %all-gather.13.cloned.1.call-done = bf16[2048,1024]{1,0:T(8,128)(2,1)} async-done(((bf16[512,1024]{1,0:T(8,128)(2,1)}), bf16[2048,1024]{1,0:T(8,128)(2,1)}) %all-gather.13.cloned.1.call-update) | async-done | bytes 4194320 | tf_op jit(solution)/shard_map/all_gather | solution.py:12
  289.9 4.4 reduce_sum.399
  299.7 3.5 fusion.155
  304.2 2.3 fusion.80
  306.5 4.7 fusion.83
  311.5 45.5 %all-reduce.6.cloned.1.call-done = bf16[512,1024]{1,0:T(8,128)(2,1)} async-done(((bf16[512,1024]{1,0:T(8,128)(2,1)}), bf16[512,1024]{1,0:T(8,128)(2,1)}) %all-reduce.6.cloned.1.call-update) | async-done | bytes 1048592 | tf_op jit(solution)/shard_map/psum | solution.py:76
  357.0 2.5 fusion.20
  360.9 78.1 %all-gather.15.cloned.1.call-done = bf16[2048,1024]{1,0:T(8,128)(2,1)} async-done(((bf16[512,1024]{1,0:T(8,128)(2,1)}), bf16[2048,1024]{1,0:T(8,128)(2,1)}) %all-gather.15.cloned.1.call-update) | async-done | bytes 4194320 | tf_op jit(solution)/shard_map/all_gather | solution.py:12
  439.0 4.4 reduce_sum.405
  443.4 4.0 fusion.144
  461.1 3.6 bitcast_convert_fusion.1
  464.9 50.5 %all-reduce.8.cloned.1.call-done = bf16[512,1024]{1,0:T(8,128)(2,1)} async-done(((bf16[512,1024]{1,0:T(8,128)(2,1)}), bf16[512,1024]{1,0:T(8,128)(2,1)}) %all-reduce.8.cloned.1.call-update) | async-done | bytes 1048592 | tf_op jit(solution)/shard_map/psum | solution.py:76
  515.3 1.8 fusion.19
  519.5 2.2 copy-done.63
  522.4 3.1 fusion.156
  526.4 2.3 fusion.74
  529.2 50.8 %all-reduce.10.cloned.1.call-done = bf16[512,1024]{1,0:T(8,128)(2,1)} async-done(((bf16[512,1024]{1,0:T(8,128)(2,1)}), bf16[512,1024]{1,0:T(8,128)(2,1)}) %all-reduce.10.cloned.1.call-update) | async-done | bytes 1048592 | tf_op jit(solution)/shard_map/psum | solution.py:76
  580.0 2.4 fusion.18
  593.8 1.8 copy.79
  595.6 1.8 copy.77
  599.2 3.6 bitcast_convert_fusion
  602.9 2.3 fusion.98
  606.8 3.7 copy.97
  610.4 2.5 copy.103
  613.0 2.3 fusion.87
  616.6 2.0 pad_maximum_fusion.2
  618.9 3.8 convert_bitcast_fusion
  624.4 2.3 pad_maximum_fusion.1
  626.7 11.4 %copy.99 = bf16[2,1024,1024]{1,0,2:T(2,128)(2,1)} copy(bf16[2,1024,1024]{2,1,0:T(8,128)(2,1)} %pad_maximum_fusion.1) | data formatting | bytes 8388608
  638.1 5.6 copy.104
  645.2 2.8 convert_bitcast_fusion.2
  649.6 2.3 pad_maximum_fusion
  658.4 1.9 fusion.34
  661.6 24.7 %all-reduce = (bf16[2,2,1024]{2,1,0:T(2,128)(2,1)S(1)}, bf16[2,2,1024]{2,1,0:T(2,128)(2,1)S(1)}, bf16[2,2,256]{2,1,0:T(2,128)(2,1)S(1)}, bf16[2,2,1024]{2,1,0:T(2,128)(2,1)S(1)}, bf16[2,1024]{1,0:T(2,128)(2,1)S(1)}) all-reduce(bf16[2,2,1024]{2,1,0:T(2,128)(2,1)S(1)} %pad_maximum_fusion.6, ...), channel_id=1, replica_groups=mesh['dp'=8,'tensor'=4] {'dp'}, use_global_device_ids=true, to_apply=%region_36.37 | all-reduce | flops 15360 | bytes 61440 | tf_op jit(solution)/shard_map/psum | solution.py:223
  689.4 3.3 add_add_fusion.4
  694.5 47.5 %reduce-scatter.9.cloned.1.call-done = bf16[2,128,3,256]{3,1,2,0:T(8,128)(2,1)} async-done(((bf16[2,1024,3,256]{3,1,2,0:T(8,128)(2,1)}), bf16[2,128,3,256]{3,1,2,0:T(8,128)(2,1)}) %reduce-scatter.9.cloned.1.call-update) | async-done | bytes 393232 | tf_op jit(solution)/shard_map/reduce_scatter | solution.py:234
  742.0 1.9 convert_element_type.288
  743.9 52.6 %reduce-scatter.15.cloned.1.call-done = bf16[128,2048]{1,0:T(8,128)(2,1)} async-done(((bf16[1024,2048]{1,0:T(8,128)(2,1)}), bf16[128,2048]{1,0:T(8,128)(2,1)}) %reduce-scatter.15.cloned.1.call-update) | async-done | bytes 524304
  799.5 51.3 %reduce-scatter.11.cloned.1.call-done = bf16[2,128,1024]{2,1,0:T(8,128)(2,1)} async-done(((bf16[2,1024,1024]{2,1,0:T(8,128)(2,1)}), bf16[2,128,1024]{2,1,0:T(8,128)(2,1)}) %reduce-scatter.11.cloned.1.call-update) | async-done | bytes 524304 | tf_op jit(solution)/shard_map/reduce_scatter | solution.py:240
  850.9 2.1 convert_element_type.294
  (300 shorter events, 87.9 us)
Async XLA Ops:
  7.2 2.6 copy-start.53
  7.2 2.6 copy-start.54
  7.2 96.3 %all-gather.9.cloned.1.call-start = ((), (), s32[]{:S(2)}) async-start(), calls=%async_computation.10 | async-start | bytes 5242880 | tf_op jit(solution)/shard_map/all_gather | solution.py:12
  7.4 6.4 copy-start.44
  9.8 191.3 %copy-start.58 = (f32[1,1,1024]{2,1,0:T(1,128)}, f32[1,1,1024]{2,1,0:T(1,128)S(1)}, u32[]{:S(2)}) copy-start(f32[1,1,1024]{2,1,0:T(1,128)S(1)} %get-tuple-element.55) | copy-start | bytes 12292
  12.5 2.7 copy-start.40
  12.6 2.6 copy-start.35
  12.6 3.3 copy-start.26
  19.9 174.2 %all-gather.11.cloned.1.call-start = ((), (), s32[]{:S(2)}) async-start(), calls=%async_computation.11 | async-start | bytes 5242880 | tf_op jit(solution)/shard_map/all_gather | solution.py:12
  106.9 2.6 copy-start.64
  109.4 2.8 copy-start.61
  114.7 175.2 %all-gather.13.cloned.1.call-start = ((), (), s32[]{:S(2)}) async-start(), calls=%async_computation.12 | async-start | bytes 5242880 | tf_op jit(solution)/shard_map/all_gather | solution.py:12
  198.5 2.7 copy-start.67
  202.5 3.2 copy-start.42
  202.6 3.1 copy-start.37
  202.6 3.7 copy-start.28
  210.5 146.5 %all-reduce.6.cloned.1.call-start = ((), (), s32[]{:S(2)}) async-start(), calls=%async_computation.4 | async-start | bytes 2097152 | tf_op jit(solution)/shard_map/psum | solution.py:76
  294.3 2.5 copy-start.65
  296.8 2.9 copy-start.62
  298.2 5.0 copy-start.73
  306.5 132.6 %all-gather.15.cloned.1.call-start = ((), (), s32[]{:S(2)}) async-start(), calls=%async_computation.13 | async-start | bytes 5242880 | tf_op jit(solution)/shard_map/all_gather | solution.py:12
  311.2 204.1 %all-reduce.8.cloned.1.call-start = ((), (), s32[]{:S(2)}) async-start(), calls=%async_computation.5 | async-start | bytes 2097152 | tf_op jit(solution)/shard_map/psum | solution.py:76
  357.0 2.6 copy-start.6
  357.0 2.8 copy-start.16
  443.4 5.4 copy-start.32
  443.4 5.9 copy-start.4
  464.8 115.2 %all-reduce.10.cloned.1.call-start = ((), (), s32[]{:S(2)}) async-start(), calls=%async_computation.6 | async-start | bytes 2097152 | tf_op jit(solution)/shard_map/psum | solution.py:76
  518.7 2.9 copy-start.63
  518.7 3.6 copy-start.70
  519.5 5.9 copy-start.23
  522.4 4.1 copy-start.66
  528.7 128.2 %all-reduce.12.cloned.1.call-start = ((), (), s32[]{:S(2)}) async-start(), calls=%async_computation.7 | async-start | bytes 2097152 | tf_op jit(solution)/shard_map/psum | solution.py:76
  580.0 2.4 copy-start.9
  580.0 2.4 copy-start.21
  584.0 3.3 copy-start.2
  585.1 3.7 copy-start.11
  602.8 89.8 %reduce-scatter.13.cloned.1.call-start = ((), (), s32[]{:S(2)}) async-start(), calls=%async_computation.14 | async-start | bytes 1179648
  610.4 2.6 copy-start.46
  610.4 2.6 copy-start.59
  612.9 129.0 %reduce-scatter.9.cloned.1.call-start = ((), (), s32[]{:S(2)}) async-start(), calls=%async_computation.8 | async-start | bytes 3538944 | tf_op jit(solution)/shard_map/reduce_scatter | solution.py:234
  618.6 4.1 copy-start.25
  618.6 177.9 %reduce-scatter.15.cloned.1.call-start = ((), (), s32[]{:S(2)}) async-start(), calls=%async_computation.15 | async-start | bytes 4718592
  618.9 3.9 copy-start.71
  643.7 207.2 %reduce-scatter.11.cloned.1.call-start = ((), (), s32[]{:S(2)}) async-start(), calls=%async_computation.9 | async-start | bytes 4718592 | tf_op jit(solution)/shard_map/reduce_scatter | solution.py:240
  645.2 2.8 copy-start.10
  645.2 2.8 copy-start.75
  652.0 2.8 copy-start.19
  658.4 31.0 %copy-start.13 = (f32[512,1024]{1,0:T(8,128)S(1)}, f32[512,1024]{1,0:T(8,128)}, u32[]{:S(2)}) copy-start(f32[512,1024]{1,0:T(8,128)} %copy-done.11) | copy-start | bytes 6291460
  (40 other events, 61.1 us)
Sparse Core Ops, SparseCore 0:
  20.0 83.4 all-gather.8
  114.8 79.2 all-gather.10
  210.7 79.2 all-gather.12
  306.6 50.3 all-reduce.5
  359.0 79.9 all-gather.14
  464.9 50.3 all-reduce.7
  528.9 51.1 all-reduce.9
  603.0 51.1 all-reduce.11
  657.3 35.3 reduce-scatter.12
  695.9 46.0 reduce-scatter.8
  745.3 51.1 reduce-scatter.14
  799.7 51.0 reduce-scatter.10
